TPU v7x, 512 devices: a whole 4x4x16 slice. The times are simulated.
512 devices in a mesh: dp: 32 (over x, y, core), expert: 16 (over z).
Axes of the slice: x: 4, y: 4, z: 16, core: 2. Of those that a mesh axis runs over, the one named last changes fastest.
Arguments:
- tokens: bfloat16 [4096, 2048], P('dp', 'expert'), may hold values from -6 to 6
- cotangent: bfloat16 [4096, 2048], P('dp', 'expert'), may hold values from -6 to 6
- expert_ids: int32 [4096, 8], P('dp'), may hold values from 0 to 127, all different within a row; in each aligned block of 128 rows (0 to 127, 128 to 255, ...) at most 16 rows name the same one
- gate_weights: float32 [4096, 8], P('dp'), may hold values from 0.05 to 1
- w_gate: bfloat16 [512, 192, 2048], P(('dp', 'expert')), may hold values from -0.125 to 0.125
- w_up: bfloat16 [512, 192, 2048], P(('dp', 'expert')), may hold values from -0.125 to 0.125
- w_down: bfloat16 [512, 192, 2048], P(('dp', 'expert')), may hold values from -0.21875 to 0.21875
Outputs:
- layer_out: bfloat16 [4096, 2048], P('dp', 'expert')
- grad_tokens: bfloat16 [4096, 2048], P('dp', 'expert')
- grad_gates: float32 [4096, 8], P('dp')
- grad_w_gate: bfloat16 [512, 192, 2048], P(('dp', 'expert'))
- grad_w_up: bfloat16 [512, 192, 2048], P(('dp', 'expert'))
- grad_w_down: bfloat16 [512, 192, 2048], P(('dp', 'expert'))
Inputs may be any that keep to these rules, and one draw needn't show every extreme that they name: `expert_ids`: each row names 8 different experts. In each aligned block of 128 rows (the rows of one index of dp) no expert is named by more than 16 rows, and in some block an expert is named by exactly 16 rows.
All inputs are finite; a program needn't handle non-finite values.
Results may differ from a plain program's by a relative error of at most 0.0064.
Values may be sent and summed in bfloat16 or wider, within the bound.
No kernel may reach another device: no remote copies, remote signals or barrier semaphores. Data moves between devices by JAX's collectives and lax.ppermute only.
A program may use at most 64 MiB of HBM per device.

v0:
```python
import jax
import jax.numpy as jnp
from jax import lax
from jax.sharding import PartitionSpec as P

SHARDS = 4


def silu_parts(preact):
    sigmoid_of = jax.nn.sigmoid(preact)
    activated = preact * sigmoid_of
    derivative = sigmoid_of * (1.0 + preact * (1.0 - sigmoid_of))
    return (activated, derivative)


def contract_last(first_op, second_op):
    return lax.dot_general(
        first_op, second_op, (((1,), (1,)), ((), ())), preferred_element_type=jnp.float32
    )


def contract_first(first_op, second_op):
    return lax.dot_general(
        first_op, second_op, (((0,), (0,)), ((), ())), preferred_element_type=jnp.float32
    )


def forward_rows(rows_x, gate_w, up_w, down_w):
    pre_gate = contract_last(rows_x, gate_w)
    pre_up = contract_last(rows_x, up_w)
    activated, derivative = silu_parts(pre_gate)
    hidden = (activated * pre_up).astype(jnp.bfloat16)
    return jnp.dot(hidden, down_w, preferred_element_type=jnp.float32).astype(jnp.bfloat16)


def backward_rows(rows_x, rows_do, gate_w, up_w, down_w):
    pre_gate = contract_last(rows_x, gate_w)
    pre_up = contract_last(rows_x, up_w)
    activated, derivative = silu_parts(pre_gate)
    hidden = (activated * pre_up).astype(jnp.bfloat16)
    d_hidden = contract_last(rows_do, down_w)
    d_pre_gate = (d_hidden * pre_up * derivative).astype(jnp.bfloat16)
    d_pre_up = (d_hidden * activated).astype(jnp.bfloat16)
    part_grad = (
        jnp.dot(d_pre_gate, gate_w, preferred_element_type=jnp.float32)
        + jnp.dot(d_pre_up, up_w, preferred_element_type=jnp.float32)
    ).astype(jnp.bfloat16)
    gradients = (
        contract_first(d_pre_gate, rows_x),
        contract_first(d_pre_up, rows_x),
        contract_first(hidden, rows_do),
    )
    return (part_grad, gradients)


def per_device(tokens, cotangent, expert_ids, gate_weights, w_gate, w_up, w_down):
    full_x, full_dy = (
        lax.all_gather(tokens, "expert", axis=1, tiled=True),
        lax.all_gather(cotangent, "expert", axis=1, tiled=True),
    )
    dp_count = lax.axis_size("dp")
    column_count = lax.axis_size("expert")
    column = lax.axis_index("expert")
    tok_count, chosen = expert_ids.shape
    features = full_x.shape[1]
    experts_all = dp_count * column_count // SHARDS
    capacity = min(tok_count, max(2, 2 * tok_count * chosen // experts_all))
    per_row = column_count // SHARDS
    assigned = tok_count * chosen
    flat_ids = expert_ids.reshape(-1)
    flat_gates = gate_weights.reshape(-1)
    owned_here = flat_ids % per_row == column // SHARDS
    target_row = flat_ids // per_row
    onehot = (
        (target_row[:, None] == jnp.arange(dp_count, dtype=jnp.int32)[None, :])
        & owned_here[:, None]
    ).astype(jnp.int32)
    rank_of = jnp.sum((jnp.cumsum(onehot, axis=0) - 1) * onehot, axis=1)
    target = jnp.where(owned_here, target_row * capacity + rank_of, dp_count * capacity)
    slot_src = (
        jnp.full((dp_count * capacity,), assigned, jnp.int32)
        .at[target]
        .set(jnp.arange(assigned, dtype=jnp.int32), mode="drop")
    )
    filled = slot_src < assigned
    safe_index = jnp.where(filled, slot_src, 0)
    slot_token = safe_index // chosen
    slot_gate = jnp.where(filled, flat_gates[safe_index], 0.0)
    slot_dy = full_dy[slot_token].astype(jnp.float32)
    send_x = jnp.where(filled[:, None], full_x[slot_token], jnp.zeros((), full_x.dtype)).reshape(
        dp_count, capacity, features
    )
    send_do = (
        (slot_gate[:, None] * slot_dy).astype(jnp.bfloat16).reshape(dp_count, capacity, features)
    )
    weights = (w_gate[0], w_up[0], w_down[0])
    recv_x = lax.all_to_all(send_x, "dp", split_axis=0, concat_axis=0, tiled=True)
    rows_x = recv_x.reshape(dp_count * capacity, features)
    expert_out = forward_rows(rows_x, *weights)
    back_out = lax.all_to_all(
        expert_out.reshape(dp_count, capacity, features),
        "dp",
        split_axis=0,
        concat_axis=0,
        tiled=True,
    )
    recv_do = lax.all_to_all(send_do, "dp", split_axis=0, concat_axis=0, tiled=True)
    rows_do = recv_do.reshape(dp_count * capacity, features)
    part_grad, gradients = backward_rows(rows_x, rows_do, *weights)
    back_grad = lax.all_to_all(
        part_grad.reshape(dp_count, capacity, features),
        "dp",
        split_axis=0,
        concat_axis=0,
        tiled=True,
    )
    width_now = back_out.shape[2]
    out_float = back_out.reshape(dp_count * capacity, width_now).astype(jnp.float32)
    grad_float = back_grad.reshape(dp_count * capacity, width_now).astype(jnp.float32)
    out_part = (
        jnp.zeros((tok_count, width_now), jnp.float32)
        .at[slot_token]
        .add(slot_gate[:, None] * out_float)
    )
    grad_part = jnp.zeros((tok_count, width_now), jnp.float32).at[slot_token].add(grad_float)
    gate_terms = jnp.sum(slot_dy * out_float, axis=1)
    gate_part = (
        jnp.zeros((assigned,), jnp.float32)
        .at[slot_src]
        .add(gate_terms, mode="drop")
        .reshape(tok_count, chosen)
    )
    out_slice, grad_slice = (
        lax.psum_scatter(out_part, "expert", scatter_dimension=1, tiled=True),
        lax.psum_scatter(grad_part, "expert", scatter_dimension=1, tiled=True),
    )
    grad_gates = lax.psum(gate_part, "expert")
    return (
        out_slice.astype(jnp.bfloat16),
        grad_slice.astype(jnp.bfloat16),
        grad_gates,
        gradients[0].astype(jnp.bfloat16)[None],
        gradients[1].astype(jnp.bfloat16)[None],
        gradients[2].astype(jnp.bfloat16)[None],
    )


def solution(mesh):
    placed = (
        P("dp", "expert"),
        P("dp", "expert"),
        P("dp", None),
        P("dp", None),
        P(("dp", "expert"), None, None),
        P(("dp", "expert"), None, None),
        P(("dp", "expert"), None, None),
    )
    return jax.shard_map(
        per_device,
        mesh=mesh,
        in_specs=placed,
        out_specs=(
            P("dp", "expert"),
            P("dp", "expert"),
            P("dp", None),
            P(("dp", "expert"), None, None),
            P(("dp", "expert"), None, None),
            P(("dp", "expert"), None, None),
        ),
        check_vma=False,
    )
```

profile of v0, /device:TPU:2, one launch (start us, length us, event | category | flops | bytes accessed | tf_op | source)
XLA Modules:
  0.0 339.8 jit_solution(6316037226412424405)
XLA Ops:
  7.2 0.0 copy-start
  7.2 0.9 copy.13
  8.0 0.1 reshape.230
  8.1 0.1 reshape.229
  8.2 0.1 reshape.228
  8.4 9.0 %reduce-window.6 = s32[32,8,128]{2,1,0:T(8,128)S(1)} reduce-window(s32[32,8,128]{2,1,0:T(8,128)S(1)} %fusion.25, s32[]{:T(128)} %constant.66.clone.1), window={size=1x1x128 pad=0_0x0_0x127_0}, to_apply=%region_0.1 | reduce-window | flops 4161536 | bytes 262148 | tf_op jit(solution)/shard_map/reduce-window
  17.5 0.1 slice.14
  17.6 0.1 copy.16
  17.7 0.1 copy.17
  17.8 0.1 add_add_fusion
  18.0 4.3 %scatter_custom_fusion = s32[512]{0:T(512)S(1)} fusion(s32[1024]{0:T(1024)S(1)} %bitcast.72, s32[1024]{0:T(1024)S(1)} %iota.11, s32[]{:T(128)} %constant.65.clone.1), kind=kCustom, calls=%fused_computation.91 | custom fusion | bytes 2052 | tf_op jit(solution)/shard_map/scatter | solution.py:83
  22.4 0.1 broadcast_in_dim.62
  22.5 38.8 %all_gather.6 = bf16[128,2048]{1,0:T(8,128)(2,1)S(1)} all-gather(bf16[128,128]{1,0:T(8,128)(2,1)} %param.7), channel_id=1, replica_groups=mesh['dp'=32,'expert'=16] {'expert'}, dimensions={1}, use_global_device_ids=true | all-gather | bytes 557056 | tf_op jit(solution)/shard_map/all_gather | solution.py:58
  61.3 2.5 gather_fusion.1
  63.7 1.6 broadcast_select_fusion
  65.3 0.0 copy-start.3
  65.3 7.8 %all-to-all-start = ((bf16[32,16,2048]{2,1,0:T(8,128)(2,1)}), bf16[32,16,2048]{2,1,0:T(8,128)(2,1)}, u32[]{:S(2)}, u32[]{:S(2)}) async-start(bf16[32,16,2048]{2,1,0:T(8,128)(2,1)} %broadcast_select_fusion), calls=%async_computation | async-start | bytes 4194304 | tf_op jit(solution)/shard_map/all_to_all | solution.py:97
  73.1 0.0 copy-done.3
  73.1 0.0 copy-start.2
  73.1 0.1 copy.18
  73.2 0.1 reshape.232
  73.3 2.3 gather_fusion
  75.7 0.1 mul.69
  75.7 0.0 copy-done.2
  75.7 28.7 %all_gather.7 = bf16[128,2048]{1,0:T(8,128)(2,1)S(1)} all-gather(bf16[128,128]{1,0:T(8,128)(2,1)S(1)} %copy-done.2), channel_id=1, replica_groups=mesh['dp'=32,'expert'=16] {'expert'}, dimensions={1}, use_global_device_ids=true | all-gather | bytes 557056 | tf_op jit(solution)/shard_map/all_gather | solution.py:59
  104.5 2.5 gather_fusion.2
  106.9 1.7 fusion
  108.6 0.0 all-to-all-done
  108.6 7.4 %all-to-all-start.2 = ((bf16[32,16,2048]{2,1,0:T(8,128)(2,1)}), bf16[32,16,2048]{2,1,0:T(8,128)(2,1)}, u32[]{:S(2)}, u32[]{:S(2)}) async-start(bf16[32,16,2048]{2,1,0:T(8,128)(2,1)} %fusion), calls=%async_computation.3 | async-start | bytes 4194304 | tf_op jit(solution)/shard_map/all_to_all | solution.py:107
  116.1 0.0 copy-start.1
  116.1 3.4 %fusion.11 = f32[512,192]{0,1:T(8,128)} fusion(bf16[512,2048]{1,0:T(8,128)(2,1)} %bitcast.5, bf16[1,192,2048]{2,1,0:T(8,128)(2,1)} %param.12), kind=kOutput, calls=%fused_computation.27 | convolution fusion | flops 402653184 | bytes 3276800 | tf_op jit(solution)/shard_map/dot_general | solution.py:17
  119.5 0.0 copy-done.1
  119.5 3.2 fusion.15
  122.7 19.4 %all-to-all-done.2 = bf16[32,16,2048]{2,1,0:T(8,128)(2,1)} async-done(((bf16[32,16,2048]{2,1,0:T(8,128)(2,1)}), bf16[32,16,2048]{2,1,0:T(8,128)(2,1)}, u32[]{:S(2)}, u32[]{:S(2)}) %all-to-all-start.2) | async-done | bytes 2097184 | tf_op jit(solution)/shard_map/all_to_all | solution.py:107
  142.1 0.0 copy-done
  142.1 2.7 multiply_convert_fusion
  144.8 2.1 convolution_convert_fusion
  146.8 7.6 %all-to-all-start.1 = ((bf16[32,16,2048]{2,1,0:T(8,128)(2,1)}), bf16[32,16,2048]{2,1,0:T(8,128)(2,1)}, u32[]{:S(2)}, u32[]{:S(2)}) async-start(bf16[32,16,2048]{2,1,0:T(8,128)(2,1)} %bitcast.67), calls=%async_computation.1 | async-start | bytes 4194304 | tf_op jit(solution)/shard_map/all_to_all | solution.py:100
  154.4 0.2 reduce-scatter.3.cloned.1.call-start
  154.7 3.8 %fusion.13 = f32[512,2048]{1,0:T(8,128)} fusion(bf16[512,192]{0,1:T(8,128)(2,1)S(1)} %get-tuple-element.15, bf16[1,192,2048]{2,1,0:T(8,128)(2,1)} %param.11), kind=kOutput, calls=%fused_computation.29 | convolution fusion | flops 402653184 | bytes 5177344 | tf_op jit(solution)/shard_map/dot_general | solution.py:45
  158.5 22.0 %all-to-all-done.1 = bf16[32,16,2048]{2,1,0:T(8,128)(2,1)} async-done(((bf16[32,16,2048]{2,1,0:T(8,128)(2,1)}), bf16[32,16,2048]{2,1,0:T(8,128)(2,1)}, u32[]{:S(2)}, u32[]{:S(2)}) %all-to-all-start.1) | async-done | bytes 2097184 | tf_op jit(solution)/shard_map/all_to_all | solution.py:100
  180.4 3.9 %bitcast_multiply_fusion = f32[512,2048]{1,0:T(8,128)} fusion(f32[512]{0:T(512)S(1)} %broadcast_select_fusion.1, bf16[32,16,2048]{2,1,0:T(8,128)(2,1)} %all-to-all-done.1), kind=kLoop, calls=%fused_computation.13 | loop fusion | flops 2097152 | bytes 6293504 | tf_op jit(solution)/shard_map/mul | solution.py:123
  184.3 9.4 %scatter_custom_fusion.1 = f32[128,2048]{1,0:T(8,128)} fusion(s32[512]{0:T(512)S(1)} %get-tuple-element.18, f32[512,2048]{1,0:T(8,128)} %bitcast_multiply_fusion, f32[]{:T(128)} %constant.64.clone.1), kind=kCustom, calls=%fused_computation.34 | custom fusion | flops 1048576 | bytes 1049088 | tf_op jit(solution)/shard_map/scatter-add | solution.py:123
  193.8 0.0 reduce-scatter.3.cloned.1.call-update
  193.8 0.0 reduce-scatter.5.cloned.1.call-start
  193.8 3.2 add_convert_fusion
  197.0 32.4 %all_to_all.20 = bf16[32,16,2048]{2,1,0:T(8,128)(2,1)} all-to-all(bf16[32,16,2048]{2,1,0:T(8,128)(2,1)S(1)} %bitcast.66), channel_id=1, replica_groups=mesh['dp'=32,'expert'=16] {'dp'}, dimensions={0} | all-to-all | bytes 4194304 | tf_op jit(solution)/shard_map/all_to_all | solution.py:110
  229.4 9.1 %scatter_custom_fusion.2 = f32[128,2048]{1,0:T(8,128)} fusion(s32[512]{0:T(512)S(1)} %get-tuple-element.18, bf16[512,2048]{1,0:T(8,128)(2,1)} %bitcast.68, f32[]{:T(128)} %constant.64.clone.1), kind=kCustom, calls=%fused_computation.11 | custom fusion | flops 2097152 | bytes 3145732 | tf_op jit(solution)/shard_map/scatter-add | solution.py:125
  238.5 0.0 reduce-scatter.5.cloned.1.call-update
  238.6 3.1 fusion.6
  241.6 3.1 fusion.5
  244.7 3.1 fusion.4
  247.8 2.2 fusion.1
  249.9 0.1 reshape.293
  250.0 3.5 %scatter_custom_fusion.3 = f32[1024]{0:T(1024)S(1)} fusion(s32[512]{0:T(512)S(1)} %get-tuple-element.17, f32[512]{0:T(512)S(1)} %reshape.293, f32[]{:T(128)} %constant.64.clone.1), kind=kCustom, calls=%fused_computation.85 | custom fusion | flops 512 | bytes 4100 | tf_op jit(solution)/shard_map/scatter-add | solution.py:130
  253.5 0.1 reshape.237
  253.6 54.9 %psum.7 = f32[128,8]{1,0:T(8,128)S(1)} all-reduce(f32[128,8]{1,0:T(8,128)S(1)} %reshape.237), channel_id=1, replica_groups=mesh['dp'=32,'expert'=16] {'expert'}, use_global_device_ids=true, to_apply=%region_10.11 | all-reduce | flops 1024 | bytes 8192 | tf_op jit(solution)/shard_map/psum | solution.py:137
  308.5 0.7 copy.19
  309.1 0.0 reduce-scatter.3.cloned.1.call-done
  309.1 1.5 convert_element_type.68
  310.6 20.9 %reduce-scatter.5.cloned.1.call-done = f32[128,128]{1,0:T(8,128)} async-done(((f32[128,2048]{1,0:T(8,128)}), f32[128,128]{1,0:T(8,128)}) %reduce-scatter.5.cloned.1.call-update) | async-done | bytes 65552 | tf_op jit(solution)/shard_map/reduce_scatter | solution.py:135
  331.5 1.5 convert_element_type.77
  (15 shorter events, 0.2 us)
Async XLA Ops:
  7.2 134.9 %copy-start = (bf16[1,192,2048]{2,1,0:T(8,128)(2,1)S(1)}, bf16[1,192,2048]{2,1,0:T(8,128)(2,1)}, u32[]{:S(2)}) copy-start(bf16[1,192,2048]{2,1,0:T(8,128)(2,1)} %param.13) | copy-start | bytes 2359300
  65.3 7.8 %copy-start.3 = (f32[128,8]{0,1:T(8,128)S(1)}, f32[128,8]{0,1:T(8,128)}, u32[]{:S(2)}) copy-start(f32[128,8]{0,1:T(8,128)} %param.10) | copy-start | bytes 12292
  65.3 43.3 %all-to-all-start = ((bf16[32,16,2048]{2,1,0:T(8,128)(2,1)}), bf16[32,16,2048]{2,1,0:T(8,128)(2,1)}, u32[]{:S(2)}, u32[]{:S(2)}) async-start(bf16[32,16,2048]{2,1,0:T(8,128)(2,1)} %broadcast_select_fusion), calls=%async_computation | async-start | bytes 4194304 | tf_op jit(solution)/shard_map/all_to_all | solution.py:97
  73.1 2.6 copy-start.2
  108.6 33.4 %all-to-all-start.2 = ((bf16[32,16,2048]{2,1,0:T(8,128)(2,1)}), bf16[32,16,2048]{2,1,0:T(8,128)(2,1)}, u32[]{:S(2)}, u32[]{:S(2)}) async-start(bf16[32,16,2048]{2,1,0:T(8,128)(2,1)} %fusion), calls=%async_computation.3 | async-start | bytes 4194304 | tf_op jit(solution)/shard_map/all_to_all | solution.py:107
  116.1 3.4 %copy-start.1 = (bf16[1,192,2048]{2,1,0:T(8,128)(2,1)S(1)}, bf16[1,192,2048]{2,1,0:T(8,128)(2,1)}, u32[]{:S(2)}) copy-start(bf16[1,192,2048]{2,1,0:T(8,128)(2,1)} %param.11) | copy-start | bytes 2359300
  146.8 33.6 %all-to-all-start.1 = ((bf16[32,16,2048]{2,1,0:T(8,128)(2,1)}), bf16[32,16,2048]{2,1,0:T(8,128)(2,1)}, u32[]{:S(2)}, u32[]{:S(2)}) async-start(bf16[32,16,2048]{2,1,0:T(8,128)(2,1)} %bitcast.67), calls=%async_computation.1 | async-start | bytes 4194304 | tf_op jit(solution)/shard_map/all_to_all | solution.py:100
  154.4 154.7 %reduce-scatter.3.cloned.1.call-start = ((), (), s32[]{:S(2)}) async-start(), calls=%async_computation.6 | async-start | bytes 1114112 | tf_op jit(solution)/shard_map/reduce_scatter | solution.py:134
  193.8 137.7 %reduce-scatter.5.cloned.1.call-start = ((), (), s32[]{:S(2)}) async-start(), calls=%async_computation.7 | async-start | bytes 1114112 | tf_op jit(solution)/shard_map/reduce_scatter | solution.py:135
Sparse Core Ops, SparseCore 0:
  193.9 66.0 reduce-scatter.2
  263.1 68.3 reduce-scatter.4
where the time goes:
time: 341 us; the launch traced here: 340 us
  blocking collectives  155 us (45%)
  waiting for transfers between devices  62.3 us (18%)
  other arithmetic  43.6 us (13%)
  matrix products  27.6 us (8%)
  starting transfers between devices  23.1 us (7%)
  between operations  14.3 us (4%)
  local copies, waits for them, and re-layouts  14.1 us (4%)
    psum x1, blocking collectives, per_device(): grad_gates = lax.psum(gate_part, 'expert')  54.9 us
    all_gather x1, blocking collectives, per_device(): lax.all_gather(tokens, 'expert', axis=1, tiled=True)  38.8 us
    all_to_all x1, blocking collectives, per_device(): lax.all_to_all(part_grad.reshape(dp_count, capacity, features), 'dp', spl...  32.4 us
    all_gather x1, blocking collectives, per_device(): lax.all_gather(cotangent, 'expert', axis=1, tiled=True)  28.7 us
    all_to_all x1, waiting for transfers between devices, per_device(): lax.all_to_all(expert_out.reshape(dp_count, capacity, features), 'dp', sp...  22 us
    reduce_scatter x1, waiting for transfers between devices, per_device(): lax.psum_scatter(grad_part, 'expert', scatter_dimension=1, tiled=True)  20.9 us
    all_to_all x1, waiting for transfers between devices, per_device(): lax.all_to_all(send_do, 'dp', split_axis=0, concat_axis=0, tiled=True)  19.4 us
    scatter-add x1, other arithmetic, per_device(): out_part = jnp.zeros((tok_count, width_now), jnp.float32).at[slot_token]....  9.44 us
  transfers between devices with their start and end apart: 5, of which 3 were waited for; matrix products, arithmetic and copies ran while one was open for 14% of the time, Pallas kernels for 0%

commit v1 on v0

--- a/solution.py
+++ b/solution.py
@@ -4,6 +4,24 @@
 from jax.sharding import PartitionSpec as P
 
 SHARDS = 4
+
+
+def gather_around(array, axis, dim):
+    ways, here, step = (lax.axis_size(axis), lax.axis_index(axis), array.shape[dim])
+    shape = [n * ways if d == dim else n for d, n in enumerate(array.shape)]
+    full = lax.dynamic_update_slice_in_dim(
+        jnp.zeros(shape, array.dtype), array, here * step, axis=dim
+    )
+    going_up = going_down = array
+    for far in range(1, ways // 2 + 1):
+        going_up = lax.ppermute(going_up, axis, [(d, (d + 1) % ways) for d in range(ways)])
+        full = lax.dynamic_update_slice_in_dim(full, going_up, (here - far) % ways * step, axis=dim)
+        if 2 * far < ways:
+            going_down = lax.ppermute(going_down, axis, [(d, (d - 1) % ways) for d in range(ways)])
+            full = lax.dynamic_update_slice_in_dim(
+                full, going_down, (here + far) % ways * step, axis=dim
+            )
+    return full
 
 
 def silu_parts(preact):
@@ -55,7 +73,7 @@
 
 def per_device(tokens, cotangent, expert_ids, gate_weights, w_gate, w_up, w_down):
     full_x, full_dy = (
-        lax.all_gather(tokens, "expert", axis=1, tiled=True),
+        gather_around(tokens, "expert", 1),
         lax.all_gather(cotangent, "expert", axis=1, tiled=True),
     )
     dp_count = lax.axis_size("dp")

time: 341 us -> 370 us (1.085)
  starting transfers between devices: 23.1 us -> 80.8 us
  blocking collectives: 155 us -> 116 us
  waiting for transfers between devices: 62.3 us -> 70.7 us
    ppermute x0 -> x15, starting transfers between devices: none -> 57.7 us  [the longest x7 42.3 us: gather_around(): lax.ppermute(going_down, axis, [(d, (d - 1) % ways) for d in range(ways)])]
    all_gather x1 -> x0, blocking collectives: 38.8 us -> none  [per_device(): lax.all_gather(tokens, 'expert', axis=1, tiled=True)]
    ppermute x0 -> x15, waiting for transfers between devices: none -> 10.1 us  [the longest x8 10.1 us: gather_around(): lax.ppermute(going_up, axis, [(d, (d + 1) % ways) for d in range(ways)])]
  transfers between devices with their start and end apart: 5 -> 20, of which waited for: 3 -> 5; matrix products, arithmetic and copies ran while one was open for 14% -> 17% of each run, Pallas kernels for 0% -> 0%
where the time goes in v1:
time: 370 us; the launch traced here: 369 us
  blocking collectives  116 us (31%)
  starting transfers between devices  80.8 us (22%)
  waiting for transfers between devices  70.7 us (19%)
  other arithmetic  43.6 us (12%)
  matrix products  28.4 us (8%)
  between operations  14.9 us (4%)
  local copies, waits for them, and re-layouts  14.4 us (4%)
    psum x1, blocking collectives, per_device(): grad_gates = lax.psum(gate_part, 'expert')  54.8 us
    ppermute x7, starting transfers between devices, gather_around(): lax.ppermute(going_down, axis, [(d, (d - 1) % ways) for d in range(ways)])  42.3 us
    all_to_all x1, blocking collectives, per_device(): lax.all_to_all(part_grad.reshape(dp_count, capacity, features), 'dp', spl...  32.4 us
    all_gather x1, blocking collectives, per_device(): lax.all_gather(cotangent, 'expert', axis=1, tiled=True)  28.7 us
    all_to_all x1, waiting for transfers between devices, per_device(): lax.all_to_all(expert_out.reshape(dp_count, capacity, features), 'dp', sp...  21.9 us
    all_to_all x1, waiting for transfers between devices, per_device(): lax.all_to_all(send_do, 'dp', split_axis=0, concat_axis=0, tiled=True)  19.4 us
    reduce_scatter x1, waiting for transfers between devices, per_device(): lax.psum_scatter(grad_part, 'expert', scatter_dimension=1, tiled=True)  19.3 us
    ppermute x8, starting transfers between devices, gather_around(): lax.ppermute(going_up, axis, [(d, (d + 1) % ways) for d in range(ways)])  15.4 us
  transfers between devices with their start and end apart: 20, of which 5 were waited for; matrix products, arithmetic and copies ran while one was open for 17% of the time, Pallas kernels for 0%

profile of v1, /device:TPU:2, one launch (start us, length us, event | category | flops | bytes accessed | tf_op | source)
XLA Modules:
  0.0 368.8 jit_solution(7368031509255788481)
XLA Ops:
  7.2 11.5 %collective-permute-start.1 = (bf16[128,128]{1,0:T(8,128)(2,1)}, bf16[128,128]{1,0:T(8,128)(2,1)S(1)}, u32[]{:S(2)}, u32[]{:S(2)}) collective-permute-start(bf16[128,128]{1,0:T(8,128)(2,1)} %param.7), channel_id=1, source_target_pairs={{0,15},{1,0},{2,1},{3,2},{4,3},{5,4},{6,5},{7,6},{8,7},{9,8},{10,9... | collective-permute-start | bytes 98312 | tf_op jit(solution)/shard_map/ppermute | solution.py:20
  18.7 1.9 collective-permute-start
  20.7 0.8 copy.13
  21.5 0.1 reshape.230
  21.5 0.1 reshape.229
  21.6 0.1 reshape.228
  21.9 9.0 %reduce-window.6 = s32[32,8,128]{2,1,0:T(8,128)S(1)} reduce-window(s32[32,8,128]{2,1,0:T(8,128)S(1)} %fusion.25, s32[]{:T(128)} %constant.149.clone.1), window={size=1x1x128 pad=0_0x0_0x127_0}, to_apply=%region_0.1 | reduce-window | flops 4161536 | bytes 262148 | tf_op jit(solution)/shard_map/reduce-window
  30.9 0.1 slice.14
  31.0 0.1 copy.16
  31.2 0.1 add_add_fusion
  31.4 4.3 %scatter_custom_fusion = s32[512]{0:T(512)S(1)} fusion(s32[1024]{0:T(1024)S(1)} %bitcast.72, s32[1024]{0:T(1024)S(1)} %iota.11, s32[]{:T(128)} %constant.148.clone.1), kind=kCustom, calls=%fused_computation.107 | custom fusion | bytes 2052 | tf_op jit(solution)/shard_map/scatter | solution.py:101
  36.1 0.1 broadcast_in_dim.65
  36.2 5.1 %collective-permute-start.3 = (bf16[128,128]{1,0:T(8,128)(2,1)S(1)}, bf16[128,128]{1,0:T(8,128)(2,1)S(1)}, u32[]{:S(2)}, u32[]{:S(2)}) collective-permute-start(bf16[128,128]{1,0:T(8,128)(2,1)S(1)} %collective-permute-done.1), channel_id=1, source_target_pairs={{0,15},{1,0},{2,1},{3,2},{4,3},{5,4},{6,5},{7,6},{8,7},{9,8},{10,9... | collective-permute-start | bytes 98312 | tf_op jit(solution)/shard_map/ppermute | solution.py:20
  41.4 1.9 collective-permute-start.2
  43.4 5.1 %collective-permute-start.5 = (bf16[128,128]{1,0:T(8,128)(2,1)S(1)}, bf16[128,128]{1,0:T(8,128)(2,1)S(1)}, u32[]{:S(2)}, u32[]{:S(2)}) collective-permute-start(bf16[128,128]{1,0:T(8,128)(2,1)S(1)} %collective-permute-done.3), channel_id=1, source_target_pairs={{0,15},{1,0},{2,1},{3,2},{4,3},{5,4},{6,5},{7,6},{8,7},{9,8},{10,9... | collective-permute-start | bytes 98312 | tf_op jit(solution)/shard_map/ppermute | solution.py:20
  48.5 1.9 collective-permute-start.4
  50.5 5.1 %collective-permute-start.7 = (bf16[128,128]{1,0:T(8,128)(2,1)S(1)}, bf16[128,128]{1,0:T(8,128)(2,1)S(1)}, u32[]{:S(2)}, u32[]{:S(2)}) collective-permute-start(bf16[128,128]{1,0:T(8,128)(2,1)S(1)} %collective-permute-done.5), channel_id=1, source_target_pairs={{0,15},{1,0},{2,1},{3,2},{4,3},{5,4},{6,5},{7,6},{8,7},{9,8},{10,9... | collective-permute-start | bytes 98312 | tf_op jit(solution)/shard_map/ppermute | solution.py:20
  55.7 1.9 collective-permute-start.6
  57.7 5.1 %collective-permute-start.9 = (bf16[128,128]{1,0:T(8,128)(2,1)S(1)}, bf16[128,128]{1,0:T(8,128)(2,1)S(1)}, u32[]{:S(2)}, u32[]{:S(2)}) collective-permute-start(bf16[128,128]{1,0:T(8,128)(2,1)S(1)} %collective-permute-done.7), channel_id=1, source_target_pairs={{0,15},{1,0},{2,1},{3,2},{4,3},{5,4},{6,5},{7,6},{8,7},{9,8},{10,9... | collective-permute-start | bytes 98312 | tf_op jit(solution)/shard_map/ppermute | solution.py:20
  62.8 1.9 collective-permute-start.8
  64.8 5.1 %collective-permute-start.11 = (bf16[128,128]{1,0:T(8,128)(2,1)S(1)}, bf16[128,128]{1,0:T(8,128)(2,1)S(1)}, u32[]{:S(2)}, u32[]{:S(2)}) collective-permute-start(bf16[128,128]{1,0:T(8,128)(2,1)S(1)} %collective-permute-done.9), channel_id=1, source_target_pairs={{0,15},{1,0},{2,1},{3,2},{4,3},{5,4},{6,5},{7,6},{8,7},{9,8},{10,9... | collective-permute-start | bytes 98312 | tf_op jit(solution)/shard_map/ppermute | solution.py:20
  69.9 1.9 collective-permute-start.10
  71.9 5.1 %collective-permute-start.13 = (bf16[128,128]{1,0:T(8,128)(2,1)S(1)}, bf16[128,128]{1,0:T(8,128)(2,1)S(1)}, u32[]{:S(2)}, u32[]{:S(2)}) collective-permute-start(bf16[128,128]{1,0:T(8,128)(2,1)S(1)} %collective-permute-done.11), channel_id=1, source_target_pairs={{0,15},{1,0},{2,1},{3,2},{4,3},{5,4},{6,5},{7,6},{8,7},{9,8},{10,9... | collective-permute-start | bytes 98312 | tf_op jit(solution)/shard_map/ppermute | solution.py:20
  77.1 1.9 collective-permute-start.12
  79.1 5.0 %collective-permute-done.12 = bf16[128,128]{1,0:T(8,128)(2,1)S(1)} collective-permute-done((bf16[128,128]{1,0:T(8,128)(2,1)S(1)}, bf16[128,128]{1,0:T(8,128)(2,1)S(1)}, u32[]{:S(2)}, u32[]{:S(2)}) %collective-permute-start.12) | collective-permute-done | bytes 32800 | tf_op jit(solution)/shard_map/ppermute | solution.py:17
  84.1 1.9 collective-permute-start.14
  86.1 5.0 %collective-permute-done.14 = bf16[128,128]{1,0:T(8,128)(2,1)S(1)} collective-permute-done((bf16[128,128]{1,0:T(8,128)(2,1)S(1)}, bf16[128,128]{1,0:T(8,128)(2,1)S(1)}, u32[]{:S(2)}, u32[]{:S(2)}) %collective-permute-start.14) | collective-permute-done | bytes 32800 | tf_op jit(solution)/shard_map/ppermute | solution.py:17
  91.1 2.5 gather_fusion.1
  93.6 1.5 broadcast_select_fusion
  95.1 7.8 %all-to-all-start = ((bf16[32,16,2048]{2,1,0:T(8,128)(2,1)}), bf16[32,16,2048]{2,1,0:T(8,128)(2,1)}, u32[]{:S(2)}, u32[]{:S(2)}) async-start(bf16[32,16,2048]{2,1,0:T(8,128)(2,1)} %broadcast_select_fusion), calls=%async_computation | async-start | bytes 4194304 | tf_op jit(solution)/shard_map/all_to_all | solution.py:115
  103.0 0.1 copy.18
  103.1 0.1 reshape.232
  103.2 2.3 gather_fusion
  105.5 0.1 mul.133
  105.6 28.7 %all_gather.3 = bf16[128,2048]{1,0:T(8,128)(2,1)S(1)} all-gather(bf16[128,128]{1,0:T(8,128)(2,1)S(1)} %copy-done.2), channel_id=1, replica_groups=mesh['dp'=32,'expert'=16] {'expert'}, dimensions={1}, use_global_device_ids=true | all-gather | bytes 557056 | tf_op jit(solution)/shard_map/all_gather | solution.py:77
  134.3 2.5 gather_fusion.2
  136.8 1.7 fusion
  138.5 7.4 %all-to-all-start.2 = ((bf16[32,16,2048]{2,1,0:T(8,128)(2,1)}), bf16[32,16,2048]{2,1,0:T(8,128)(2,1)}, u32[]{:S(2)}, u32[]{:S(2)}) async-start(bf16[32,16,2048]{2,1,0:T(8,128)(2,1)} %fusion), calls=%async_computation.3 | async-start | bytes 4194304 | tf_op jit(solution)/shard_map/all_to_all | solution.py:125
  145.9 3.4 fusion.11
  149.4 3.2 fusion.15
  152.6 19.4 %all-to-all-done.2 = bf16[32,16,2048]{2,1,0:T(8,128)(2,1)} async-done(((bf16[32,16,2048]{2,1,0:T(8,128)(2,1)}), bf16[32,16,2048]{2,1,0:T(8,128)(2,1)}, u32[]{:S(2)}, u32[]{:S(2)}) %all-to-all-start.2) | async-done | bytes 2097184 | tf_op jit(solution)/shard_map/all_to_all | solution.py:125
  171.9 3.4 multiply_convert_fusion
  175.3 2.1 convolution_convert_fusion
  177.3 7.6 %all-to-all-start.1 = ((bf16[32,16,2048]{2,1,0:T(8,128)(2,1)}), bf16[32,16,2048]{2,1,0:T(8,128)(2,1)}, u32[]{:S(2)}, u32[]{:S(2)}) async-start(bf16[32,16,2048]{2,1,0:T(8,128)(2,1)} %bitcast.67), calls=%async_computation.1 | async-start | bytes 4194304 | tf_op jit(solution)/shard_map/all_to_all | solution.py:118
  184.9 0.2 reduce-scatter.3.cloned.1.call-start
  185.2 3.8 %fusion.13 = f32[512,2048]{1,0:T(8,128)} fusion(bf16[512,192]{0,1:T(8,128)(2,1)S(1)} %get-tuple-element.15, bf16[1,192,2048]{2,1,0:T(8,128)(2,1)} %param.11), kind=kOutput, calls=%fused_computation.29 | convolution fusion | flops 402653184 | bytes 5177344 | tf_op jit(solution)/shard_map/dot_general | solution.py:63
  189.0 21.9 %all-to-all-done.1 = bf16[32,16,2048]{2,1,0:T(8,128)(2,1)} async-done(((bf16[32,16,2048]{2,1,0:T(8,128)(2,1)}), bf16[32,16,2048]{2,1,0:T(8,128)(2,1)}, u32[]{:S(2)}, u32[]{:S(2)}) %all-to-all-start.1) | async-done | bytes 2097184 | tf_op jit(solution)/shard_map/all_to_all | solution.py:118
  210.9 3.9 %bitcast_multiply_fusion = f32[512,2048]{1,0:T(8,128)} fusion(f32[512]{0:T(512)S(1)} %broadcast_select_fusion.1, bf16[32,16,2048]{2,1,0:T(8,128)(2,1)} %all-to-all-done.1), kind=kLoop, calls=%fused_computation.13 | loop fusion | flops 2097152 | bytes 6293504 | tf_op jit(solution)/shard_map/mul | solution.py:141
  214.8 9.5 %scatter_custom_fusion.1 = f32[128,2048]{1,0:T(8,128)} fusion(s32[512]{0:T(512)S(1)} %get-tuple-element.18, f32[512,2048]{1,0:T(8,128)} %bitcast_multiply_fusion, f32[]{:T(128)} %constant.147.clone.1), kind=kCustom, calls=%fused_computation.34 | custom fusion | flops 1048576 | bytes 1049088 | tf_op jit(solution)/shard_map/scatter-add | solution.py:141
  224.4 3.2 add_convert_fusion
  227.6 32.4 %all_to_all.20 = bf16[32,16,2048]{2,1,0:T(8,128)(2,1)} all-to-all(bf16[32,16,2048]{2,1,0:T(8,128)(2,1)S(1)} %bitcast.66), channel_id=1, replica_groups=mesh['dp'=32,'expert'=16] {'dp'}, dimensions={0} | all-to-all | bytes 4194304 | tf_op jit(solution)/shard_map/all_to_all | solution.py:128
  260.0 9.1 %scatter_custom_fusion.2 = f32[128,2048]{1,0:T(8,128)} fusion(s32[512]{0:T(512)S(1)} %get-tuple-element.18, bf16[512,2048]{1,0:T(8,128)(2,1)} %bitcast.68, f32[]{:T(128)} %constant.147.clone.1), kind=kCustom, calls=%fused_computation.11 | custom fusion | flops 2097152 | bytes 3145732 | tf_op jit(solution)/shard_map/scatter-add | solution.py:143
  269.1 3.1 fusion.6
  272.2 3.2 fusion.5
  275.4 3.1 fusion.4
  278.4 2.2 fusion.1
  280.6 0.1 reshape.293
  280.7 3.5 scatter_custom_fusion.3
  284.2 0.1 reshape.237
  284.3 54.8 %psum.7 = f32[128,8]{1,0:T(8,128)S(1)} all-reduce(f32[128,8]{1,0:T(8,128)S(1)} %reshape.237), channel_id=1, replica_groups=mesh['dp'=32,'expert'=16] {'expert'}, use_global_device_ids=true, to_apply=%region_10.11 | all-reduce | flops 1024 | bytes 8192 | tf_op jit(solution)/shard_map/psum | solution.py:155
  339.1 0.7 copy.19
  339.8 1.5 convert_element_type.68
  341.2 19.3 %reduce-scatter.5.cloned.1.call-done = f32[128,128]{1,0:T(8,128)} async-done(((f32[128,2048]{1,0:T(8,128)}), f32[128,128]{1,0:T(8,128)}) %reduce-scatter.5.cloned.1.call-update) | async-done | bytes 65552 | tf_op jit(solution)/shard_map/reduce_scatter | solution.py:153
  360.5 1.5 convert_element_type.77
  (61 shorter events, 0.8 us)
Async XLA Ops:
  7.2 164.8 %copy-start = (bf16[1,192,2048]{2,1,0:T(8,128)(2,1)S(1)}, bf16[1,192,2048]{2,1,0:T(8,128)(2,1)}, u32[]{:S(2)}) copy-start(bf16[1,192,2048]{2,1,0:T(8,128)(2,1)} %param.13) | copy-start | bytes 2359300
  7.2 28.6 %copy-start.3 = (bf16[128,128]{1,0:T(8,128)(2,1)S(1)}, bf16[128,128]{1,0:T(8,128)(2,1)}, u32[]{:S(2)}) copy-start(bf16[128,128]{1,0:T(8,128)(2,1)} %param.7) | copy-start | bytes 98308
  7.2 29.0 %collective-permute-start.1 = (bf16[128,128]{1,0:T(8,128)(2,1)}, bf16[128,128]{1,0:T(8,128)(2,1)S(1)}, u32[]{:S(2)}, u32[]{:S(2)}) collective-permute-start(bf16[128,128]{1,0:T(8,128)(2,1)} %param.7), channel_id=1, source_target_pairs={{0,15},{1,0},{2,1},{3,2},{4,3},{5,4},{6,5},{7,6},{8,7},{9,8},{10,9... | collective-permute-start | bytes 98312 | tf_op jit(solution)/shard_map/ppermute | solution.py:20
  18.7 22.7 %collective-permute-start = (bf16[128,128]{1,0:T(8,128)(2,1)}, bf16[128,128]{1,0:T(8,128)(2,1)S(1)}, u32[]{:S(2)}, u32[]{:S(2)}) collective-permute-start(bf16[128,128]{1,0:T(8,128)(2,1)} %param.7), channel_id=1, source_target_pairs={{0,1},{1,2},{2,3},{3,4},{4,5},{5,6},{6,7},{7,8},{8,9},{9,10},{10,1... | collective-permute-start | bytes 98312 | tf_op jit(solution)/shard_map/ppermute | solution.py:17
  36.2 7.1 %collective-permute-start.3 = (bf16[128,128]{1,0:T(8,128)(2,1)S(1)}, bf16[128,128]{1,0:T(8,128)(2,1)S(1)}, u32[]{:S(2)}, u32[]{:S(2)}) collective-permute-start(bf16[128,128]{1,0:T(8,128)(2,1)S(1)} %collective-permute-done.1), channel_id=1, source_target_pairs={{0,15},{1,0},{2,1},{3,2},{4,3},{5,4},{6,5},{7,6},{8,7},{9,8},{10,9... | collective-permute-start | bytes 98312 | tf_op jit(solution)/shard_map/ppermute | solution.py:20
  41.4 7.1 %collective-permute-start.2 = (bf16[128,128]{1,0:T(8,128)(2,1)S(1)}, bf16[128,128]{1,0:T(8,128)(2,1)S(1)}, u32[]{:S(2)}, u32[]{:S(2)}) collective-permute-start(bf16[128,128]{1,0:T(8,128)(2,1)S(1)} %collective-permute-done), channel_id=1, source_target_pairs={{0,1},{1,2},{2,3},{3,4},{4,5},{5,6},{6,7},{7,8},{8,9},{9,10},{10,1... | collective-permute-start | bytes 98312 | tf_op jit(solution)/shard_map/ppermute | solution.py:17
  43.4 7.1 %collective-permute-start.5 = (bf16[128,128]{1,0:T(8,128)(2,1)S(1)}, bf16[128,128]{1,0:T(8,128)(2,1)S(1)}, u32[]{:S(2)}, u32[]{:S(2)}) collective-permute-start(bf16[128,128]{1,0:T(8,128)(2,1)S(1)} %collective-permute-done.3), channel_id=1, source_target_pairs={{0,15},{1,0},{2,1},{3,2},{4,3},{5,4},{6,5},{7,6},{8,7},{9,8},{10,9... | collective-permute-start | bytes 98312 | tf_op jit(solution)/shard_map/ppermute | solution.py:20
  48.5 7.1 %collective-permute-start.4 = (bf16[128,128]{1,0:T(8,128)(2,1)S(1)}, bf16[128,128]{1,0:T(8,128)(2,1)S(1)}, u32[]{:S(2)}, u32[]{:S(2)}) collective-permute-start(bf16[128,128]{1,0:T(8,128)(2,1)S(1)} %collective-permute-done.2), channel_id=1, source_target_pairs={{0,1},{1,2},{2,3},{3,4},{4,5},{5,6},{6,7},{7,8},{8,9},{9,10},{10,1... | collective-permute-start | bytes 98312 | tf_op jit(solution)/shard_map/ppermute | solution.py:17
  50.5 7.1 %collective-permute-start.7 = (bf16[128,128]{1,0:T(8,128)(2,1)S(1)}, bf16[128,128]{1,0:T(8,128)(2,1)S(1)}, u32[]{:S(2)}, u32[]{:S(2)}) collective-permute-start(bf16[128,128]{1,0:T(8,128)(2,1)S(1)} %collective-permute-done.5), channel_id=1, source_target_pairs={{0,15},{1,0},{2,1},{3,2},{4,3},{5,4},{6,5},{7,6},{8,7},{9,8},{10,9... | collective-permute-start | bytes 98312 | tf_op jit(solution)/shard_map/ppermute | solution.py:20
  55.7 7.1 %collective-permute-start.6 = (bf16[128,128]{1,0:T(8,128)(2,1)S(1)}, bf16[128,128]{1,0:T(8,128)(2,1)S(1)}, u32[]{:S(2)}, u32[]{:S(2)}) collective-permute-start(bf16[128,128]{1,0:T(8,128)(2,1)S(1)} %collective-permute-done.4), channel_id=1, source_target_pairs={{0,1},{1,2},{2,3},{3,4},{4,5},{5,6},{6,7},{7,8},{8,9},{9,10},{10,1... | collective-permute-start | bytes 98312 | tf_op jit(solution)/shard_map/ppermute | solution.py:17
  57.7 7.1 %collective-permute-start.9 = (bf16[128,128]{1,0:T(8,128)(2,1)S(1)}, bf16[128,128]{1,0:T(8,128)(2,1)S(1)}, u32[]{:S(2)}, u32[]{:S(2)}) collective-permute-start(bf16[128,128]{1,0:T(8,128)(2,1)S(1)} %collective-permute-done.7), channel_id=1, source_target_pairs={{0,15},{1,0},{2,1},{3,2},{4,3},{5,4},{6,5},{7,6},{8,7},{9,8},{10,9... | collective-permute-start | bytes 98312 | tf_op jit(solution)/shard_map/ppermute | solution.py:20
  62.8 7.1 %collective-permute-start.8 = (bf16[128,128]{1,0:T(8,128)(2,1)S(1)}, bf16[128,128]{1,0:T(8,128)(2,1)S(1)}, u32[]{:S(2)}, u32[]{:S(2)}) collective-permute-start(bf16[128,128]{1,0:T(8,128)(2,1)S(1)} %collective-permute-done.6), channel_id=1, source_target_pairs={{0,1},{1,2},{2,3},{3,4},{4,5},{5,6},{6,7},{7,8},{8,9},{9,10},{10,1... | collective-permute-start | bytes 98312 | tf_op jit(solution)/shard_map/ppermute | solution.py:17
  64.8 7.1 %collective-permute-start.11 = (bf16[128,128]{1,0:T(8,128)(2,1)S(1)}, bf16[128,128]{1,0:T(8,128)(2,1)S(1)}, u32[]{:S(2)}, u32[]{:S(2)}) collective-permute-start(bf16[128,128]{1,0:T(8,128)(2,1)S(1)} %collective-permute-done.9), channel_id=1, source_target_pairs={{0,15},{1,0},{2,1},{3,2},{4,3},{5,4},{6,5},{7,6},{8,7},{9,8},{10,9... | collective-permute-start | bytes 98312 | tf_op jit(solution)/shard_map/ppermute | solution.py:20
  69.9 7.1 %collective-permute-start.10 = (bf16[128,128]{1,0:T(8,128)(2,1)S(1)}, bf16[128,128]{1,0:T(8,128)(2,1)S(1)}, u32[]{:S(2)}, u32[]{:S(2)}) collective-permute-start(bf16[128,128]{1,0:T(8,128)(2,1)S(1)} %collective-permute-done.8), channel_id=1, source_target_pairs={{0,1},{1,2},{2,3},{3,4},{4,5},{5,6},{6,7},{7,8},{8,9},{9,10},{10,1... | collective-permute-start | bytes 98312 | tf_op jit(solution)/shard_map/ppermute | solution.py:17
  71.9 14.1 %collective-permute-start.13 = (bf16[128,128]{1,0:T(8,128)(2,1)S(1)}, bf16[128,128]{1,0:T(8,128)(2,1)S(1)}, u32[]{:S(2)}, u32[]{:S(2)}) collective-permute-start(bf16[128,128]{1,0:T(8,128)(2,1)S(1)} %collective-permute-done.11), channel_id=1, source_target_pairs={{0,15},{1,0},{2,1},{3,2},{4,3},{5,4},{6,5},{7,6},{8,7},{9,8},{10,9... | collective-permute-start | bytes 98312 | tf_op jit(solution)/shard_map/ppermute | solution.py:20
  77.1 7.0 %collective-permute-start.12 = (bf16[128,128]{1,0:T(8,128)(2,1)S(1)}, bf16[128,128]{1,0:T(8,128)(2,1)S(1)}, u32[]{:S(2)}, u32[]{:S(2)}) collective-permute-start(bf16[128,128]{1,0:T(8,128)(2,1)S(1)} %collective-permute-done.10), channel_id=1, source_target_pairs={{0,1},{1,2},{2,3},{3,4},{4,5},{5,6},{6,7},{7,8},{8,9},{9,10},{10,1... | collective-permute-start | bytes 98312 | tf_op jit(solution)/shard_map/ppermute | solution.py:17
  84.1 7.0 %collective-permute-start.14 = (bf16[128,128]{1,0:T(8,128)(2,1)S(1)}, bf16[128,128]{1,0:T(8,128)(2,1)S(1)}, u32[]{:S(2)}, u32[]{:S(2)}) collective-permute-start(bf16[128,128]{1,0:T(8,128)(2,1)S(1)} %collective-permute-done.12), channel_id=1, source_target_pairs={{0,1},{1,2},{2,3},{3,4},{4,5},{5,6},{6,7},{7,8},{8,9},{9,10},{10,1... | collective-permute-start | bytes 98312 | tf_op jit(solution)/shard_map/ppermute | solution.py:17
  95.1 7.8 %copy-start.4 = (f32[128,8]{0,1:T(8,128)S(1)}, f32[128,8]{0,1:T(8,128)}, u32[]{:S(2)}) copy-start(f32[128,8]{0,1:T(8,128)} %param.10) | copy-start | bytes 12292
  95.1 43.3 %all-to-all-start = ((bf16[32,16,2048]{2,1,0:T(8,128)(2,1)}), bf16[32,16,2048]{2,1,0:T(8,128)(2,1)}, u32[]{:S(2)}, u32[]{:S(2)}) async-start(bf16[32,16,2048]{2,1,0:T(8,128)(2,1)} %broadcast_select_fusion), calls=%async_computation | async-start | bytes 4194304 | tf_op jit(solution)/shard_map/all_to_all | solution.py:115
  103.0 2.6 copy-start.2
  138.5 33.4 %all-to-all-start.2 = ((bf16[32,16,2048]{2,1,0:T(8,128)(2,1)}), bf16[32,16,2048]{2,1,0:T(8,128)(2,1)}, u32[]{:S(2)}, u32[]{:S(2)}) async-start(bf16[32,16,2048]{2,1,0:T(8,128)(2,1)} %fusion), calls=%async_computation.3 | async-start | bytes 4194304 | tf_op jit(solution)/shard_map/all_to_all | solution.py:125
  145.9 3.4 copy-start.1
  177.3 33.6 %all-to-all-start.1 = ((bf16[32,16,2048]{2,1,0:T(8,128)(2,1)}), bf16[32,16,2048]{2,1,0:T(8,128)(2,1)}, u32[]{:S(2)}, u32[]{:S(2)}) async-start(bf16[32,16,2048]{2,1,0:T(8,128)(2,1)} %bitcast.67), calls=%async_computation.1 | async-start | bytes 4194304 | tf_op jit(solution)/shard_map/all_to_all | solution.py:118
  184.9 154.8 %reduce-scatter.3.cloned.1.call-start = ((), (), s32[]{:S(2)}) async-start(), calls=%async_computation.6 | async-start | bytes 1114112 | tf_op jit(solution)/shard_map/reduce_scatter | solution.py:152
  224.3 136.2 %reduce-scatter.5.cloned.1.call-start = ((), (), s32[]{:S(2)}) async-start(), calls=%async_computation.7 | async-start | bytes 1114112 | tf_op jit(solution)/shard_map/reduce_scatter | solution.py:153
Sparse Core Ops, SparseCore 0:
  224.4 64.7 reduce-scatter.2
  292.3 68.1 reduce-scatter.4
